TPU v7x, 32 devices: a whole 2x2x4 slice. The times are simulated.
32 devices in a mesh: grp: 4 (over x, core), sub: 8 (over z, y).
Axes of the slice: x: 2, y: 2, z: 4, core: 2. Of those that a mesh axis runs over, the one named last changes fastest.
Arguments:
- shell_state: float32 [2, 48, 262144], P(None, None, ('grp', 'sub')), may hold values from -6 to 6
- source: bfloat16 [2, 256, 16, 768], P(None, ('grp', 'sub')), may hold values from -6 to 6
- knockdown: bfloat16 [256, 16, 768], P(('grp', 'sub')), may hold values from 0.29882812 to 3
- orient: int32 [256, 48], P(('grp', 'sub')), may hold values from 0 to 3
- active: int32 [256], P(('grp', 'sub')), may hold values from 24 to 48
- point_owner: int32 [256, 64], P(('grp', 'sub')), may hold values from 0 to 31, as said below
- owner_nodes: int32 [32, 32, 32], P(('grp', 'sub')), may hold values from -1 to 8191, as said below
Outputs:
- adjoint: float32 [2, 256, 16, 768], P(None, ('grp', 'sub'))
- shell_force: float32 [2, 48, 262144], P(None, None, ('grp', 'sub'))
Inputs may be any that keep to these rules, and one draw needn't show every extreme that they name: `point_owner`: within every block of boundary columns (see the steps), no owner appears more than 32 times, and in every draw one owner, the same for all blocks, appears exactly 32 times in each block. owner_nodes[o, d, r] is the local node of the column of block d with owner o that has r earlier such columns, and -1 for r at or beyond the count of such columns.
All inputs are finite; a program needn't handle non-finite values.
Results may differ from a plain program's by a relative error of at most 0.0003.
Values sent between devices are 32-bit elements; how exact they have to be, the bound alone decides.
No kernel may reach another device: no remote copies, remote signals or barrier semaphores. Data moves between devices by JAX's collectives and lax.ppermute only.
A program may use at most 64 MiB of HBM per device.

v0:
```python
import math
import jax
import jax.numpy as jnp
from jax import lax
from jax.sharding import PartitionSpec as P

SWEEPS = 3
STEPS = 2
FIBER_COND = 1.0
TRANSVERSE = 0.25
THROUGH = 0.15
MASS_SHARE = 0.05
CHEB_CENTER = 1.02
CHEB_HALF = 0.98


def face_mean(lower_side, upper_side):
    return jnp.where((lower_side > 0) & (upper_side > 0), 0.5 * (lower_side + upper_side), 0.0)


def flat_coeffs(knock_flat, orient, active, side_cells):
    sub_count, side_x, flat_width = knock_flat.shape
    ply_count = orient.shape[1]
    active_mask = (jnp.arange(ply_count)[None, :] < active[:, None]).astype(jnp.float32)
    ply_angle = orient.astype(jnp.float32) * (math.pi / 6.0)
    cos_square = jnp.cos(ply_angle) ** 2
    fiber_part = (FIBER_COND * cos_square + TRANSVERSE * (1.0 - cos_square)) * active_mask
    cross_part = (FIBER_COND * (1.0 - cos_square) + TRANSVERSE * cos_square) * active_mask
    fiber_flat = jnp.repeat(fiber_part, side_cells, axis=1)[:, None, :]
    cross_flat = jnp.repeat(cross_part, side_cells, axis=1)[:, None, :]
    mask_flat = jnp.repeat(active_mask, side_cells, axis=1)[:, None, :]
    along_x = knock_flat * fiber_flat
    along_y = knock_flat * cross_flat
    across_ply = knock_flat * (THROUGH * mask_flat)
    flat_place = jnp.arange(flat_width)
    y_place = (flat_place % side_cells)[None, None, :]
    ply_place = (flat_place // side_cells)[None, None, :]
    x_place = jnp.arange(side_x)[None, :, None]
    face_west = jnp.where(x_place == 0, 0.0, face_mean(jnp.roll(along_x, 1, axis=1), along_x))
    face_east = jnp.where(
        x_place == side_x - 1, 0.0, face_mean(along_x, jnp.roll(along_x, -1, axis=1))
    )
    face_south = jnp.where(y_place == 0, 0.0, face_mean(jnp.roll(along_y, 1, axis=2), along_y))
    face_north = jnp.where(
        y_place == side_cells - 1, 0.0, face_mean(along_y, jnp.roll(along_y, -1, axis=2))
    )
    face_below = jnp.where(
        ply_place == 0, 0.0, face_mean(jnp.roll(across_ply, side_cells, axis=2), across_ply)
    )
    face_above = jnp.where(
        ply_place == ply_count - 1,
        0.0,
        face_mean(across_ply, jnp.roll(across_ply, -side_cells, axis=2)),
    )
    ghost_west = jnp.where(x_place == 0, along_x, 0.0)
    ghost_east = jnp.where(x_place == side_x - 1, along_x, 0.0)
    ghost_south = jnp.where(y_place == 0, along_y, 0.0)
    ghost_north = jnp.where(y_place == side_cells - 1, along_y, 0.0)
    diagonal = (
        face_west
        + face_east
        + face_south
        + face_north
        + face_below
        + face_above
        + ghost_west
        + ghost_east
        + ghost_south
        + ghost_north
        + MASS_SHARE * (along_x + along_y + across_ply)
        + (1.0 - mask_flat)
    )
    return (
        face_west,
        face_east,
        face_south,
        face_north,
        face_below,
        face_above,
        ghost_west,
        ghost_east,
        ghost_south,
        ghost_north,
        diagonal,
        mask_flat,
    )


def operate_flat(field_in, coeffs, side_cells):
    face_west, face_east, face_south, face_north, face_below, face_above = coeffs[:6]
    diagonal = coeffs[10]
    beside = (
        face_west * jnp.roll(field_in, 1, axis=2)
        + face_east * jnp.roll(field_in, -1, axis=2)
        + face_south * jnp.roll(field_in, 1, axis=3)
        + face_north * jnp.roll(field_in, -1, axis=3)
        + face_below * jnp.roll(field_in, side_cells, axis=3)
        + face_above * jnp.roll(field_in, -side_cells, axis=3)
    )
    return diagonal * field_in - beside


def solve_cells(source, knockdown, orient, active, ghosts):
    case_count, sub_count, side_x, flat_width = source.shape
    ply_count = orient.shape[1]
    side_cells = flat_width // ply_count
    coeffs = flat_coeffs(knockdown.astype(jnp.float32), orient, active, side_cells)
    ghost_west, ghost_east, ghost_south, ghost_north, diagonal, mask_flat = coeffs[6:]
    value_west = ghosts[:, :, :, 0:side_cells].reshape(case_count, sub_count, 1, flat_width)
    value_east = ghosts[:, :, :, side_cells : 2 * side_cells].reshape(
        case_count, sub_count, 1, flat_width
    )
    value_south = jnp.repeat(
        jnp.swapaxes(ghosts[:, :, :, 2 * side_cells : 3 * side_cells], 2, 3), side_cells, axis=3
    )
    value_north = jnp.repeat(
        jnp.swapaxes(ghosts[:, :, :, 3 * side_cells :], 2, 3), side_cells, axis=3
    )
    field_cells = source.astype(jnp.float32)
    residual = (
        mask_flat * field_cells
        + ghost_west * value_west
        + ghost_east * value_east
        + ghost_south * value_south
        + ghost_north * value_north
    )
    adjoint = jnp.zeros_like(residual)
    sigma_ratio = CHEB_CENTER / CHEB_HALF
    for sweep_index in range(SWEEPS):
        rho_now = 1.0 / sigma_ratio
        direction = residual / (CHEB_CENTER * diagonal)
        for step_index in range(STEPS):
            adjoint = adjoint + direction
            if not (sweep_index + 1 == SWEEPS and step_index + 1 == STEPS):
                residual = residual - operate_flat(direction, coeffs, side_cells)
            if step_index + 1 < STEPS:
                rho_next = 1.0 / (2.0 * sigma_ratio - rho_now)
                direction = rho_next * rho_now * direction + 2.0 * rho_next / CHEB_HALF * (
                    residual / diagonal
                )
                rho_now = rho_next
    force_west = jnp.sum(ghost_west * (value_west - adjoint), axis=2).reshape(
        case_count, sub_count, ply_count, side_cells
    )
    force_east = jnp.sum(ghost_east * (value_east - adjoint), axis=2).reshape(
        case_count, sub_count, ply_count, side_cells
    )
    south_term = (ghost_south * (value_south - adjoint)).reshape(
        case_count, sub_count, side_x, ply_count, side_cells
    )
    north_term = (ghost_north * (value_north - adjoint)).reshape(
        case_count, sub_count, side_x, ply_count, side_cells
    )
    force_south = jnp.swapaxes(jnp.sum(south_term, axis=4), 2, 3)
    force_north = jnp.swapaxes(jnp.sum(north_term, axis=4), 2, 3)
    forces = jnp.concatenate([force_west, force_east, force_south, force_north], axis=3)
    return (adjoint, forces)


def per_device(shell_state, source, knockdown, orient, active, point_owner, owner_nodes):
    case_count, sub_local, side_x, flat_width = source.shape
    ply_count = orient.shape[1]
    node_local = shell_state.shape[2]
    groups = lax.axis_size("grp")
    tile_count = lax.axis_size("sub")
    devices = groups * tile_count
    slot_depth = owner_nodes.shape[2]
    slot_total = devices * slot_depth
    boundary_width = point_owner.shape[1]
    row_count = sub_local * boundary_width
    node_table = owner_nodes[0]
    live_slot = node_table >= 0
    picked = jnp.where(
        live_slot[None, None], shell_state[:, :, jnp.where(live_slot, node_table, 0)], 0.0
    )
    owners = point_owner.reshape(row_count)
    owner_hit = (owners[:, None] == jnp.arange(devices, dtype=jnp.int32)[None, :]).astype(jnp.int32)
    slot_rank = jnp.sum((jnp.cumsum(owner_hit, axis=0) - owner_hit) * owner_hit, axis=1)
    slot_index = owners * slot_depth + slot_rank
    slot_source = (
        jnp.full((slot_total,), row_count, jnp.int32)
        .at[slot_index]
        .set(jnp.arange(row_count, dtype=jnp.int32))
    )
    arrived = lax.all_to_all(
        picked.reshape(case_count, ply_count, slot_total),
        ("grp", "sub"),
        split_axis=2,
        concat_axis=2,
        tiled=True,
    )
    values = arrived[:, :, slot_index]
    ghosts = jnp.transpose(
        values.reshape(case_count, ply_count, sub_local, boundary_width), (0, 2, 1, 3)
    )

    def solve_one(sub_index):
        sub_source = lax.dynamic_slice_in_dim(source, sub_index, 1, 1)
        sub_knock = lax.dynamic_slice_in_dim(knockdown, sub_index, 1, 0)
        sub_orient = lax.dynamic_slice_in_dim(orient, sub_index, 1, 0)
        sub_active = lax.dynamic_slice_in_dim(active, sub_index, 1, 0)
        sub_ghosts = lax.dynamic_slice_in_dim(ghosts, sub_index, 1, 1)
        return solve_cells(sub_source, sub_knock, sub_orient, sub_active, sub_ghosts)

    adjoint, forces = lax.map(solve_one, jnp.arange(sub_local))
    adjoint = jnp.moveaxis(adjoint[:, :, 0], 0, 1)
    force_rows = jnp.transpose(forces[:, :, 0], (0, 2, 3, 1)).reshape(
        sub_local * boundary_width, case_count * ply_count
    )
    force_rows = jnp.transpose(forces[:, :, 0], (0, 3, 1, 2)).reshape(
        row_count, case_count * ply_count
    )
    padded_rows = jnp.concatenate(
        [force_rows, jnp.zeros((1, case_count * ply_count), jnp.float32)], axis=0
    )
    outbound = padded_rows[slot_source].T.reshape(case_count, ply_count, slot_total)
    returned = lax.all_to_all(outbound, ("grp", "sub"), split_axis=2, concat_axis=2, tiled=True)
    returned_rows = returned.reshape(case_count * ply_count, slot_total).T
    target = jnp.where(live_slot, node_table, node_local).reshape(slot_total)
    node_rows = (
        jnp.zeros((node_local, case_count * ply_count), jnp.float32)
        .at[target]
        .add(returned_rows, mode="drop")
    )
    shell_force = node_rows.T.reshape(case_count, ply_count, node_local)
    return (adjoint, shell_force)


def solution(mesh):
    in_specs = (
        P(None, None, ("grp", "sub")),
        P(None, ("grp", "sub"), None, None),
        P(("grp", "sub"), None, None),
        P(("grp", "sub"), None),
        P(("grp", "sub")),
        P(("grp", "sub"), None),
        P(("grp", "sub"), None, None),
    )
    out_specs = (P(None, ("grp", "sub"), None, None), P(None, None, ("grp", "sub")))
    return jax.shard_map(
        per_device, mesh=mesh, in_specs=in_specs, out_specs=out_specs, check_vma=False
    )
```

profile of v0, /device:TPU:0, one launch (start us, length us, event | category | flops | bytes accessed | tf_op | source)
XLA Modules:
  0.0 206.3 jit_solution(701925207366598028)
XLA Ops:
  0.6 0.7 compare_select_fusion.2
  1.4 0.7 broadcast_compare_fusion
  2.1 10.7 %copy.32 = f32[2,48,8192]{1,0,2:T(2,128)} copy(f32[2,48,8192]{2,1,0:T(8,128)} %param.9) | data formatting | bytes 6291456 | tf_op args[0]
  12.9 6.9 %gather_fusion = f32[1024,2,48]{2,1,0:T(2,128)S(1)} fusion(f32[2,48,8192]{1,0,2:T(2,128)} %copy.32, s32[1024]{0:T(1024)S(1)} %broadcast_clamp_fusion), kind=kCustom, calls=%fused_computation | custom fusion | bytes 790528 | tf_op jit(solution)/shard_map/gather | solution.py:174
  19.8 1.0 copy.47
  20.8 0.9 copy.48
  21.8 3.7 %bitcast_select_fusion = f32[2,48,1024]{1,0,2:T(2,128)S(1)} fusion(f32[2,48,32,32]{1,0,3,2:T(2,128)S(1)} %copy.48, pred[1024]{0:T(1024)(128)(4,1)S(1)} %ge.30), kind=kLoop, calls=%fused_computation.174 | loop fusion | flops 98304 | bytes 787456 | tf_op jit(solution)/shard_map/jit(_where)/select_n | solution.py:173
  25.5 2.6 %reshape.1631 = f32[32,1,3072]{2,1,0:T(1,128)} reshape(f32[1024,2,48]{2,1,0:T(2,128)S(1)} %bitcast.161) | data formatting | bytes 786432
  28.1 7.3 %all-to-all-start = ((f32[32,1,3072]{2,1,0:T(1,128)}), f32[32,1,3072]{2,1,0:T(1,128)S(1)}, u32[]{:S(2)}, u32[]{:S(2)}) async-start(f32[32,1,3072]{2,1,0:T(1,128)} %reshape.1631), calls=%async_computation | async-start | bytes 786432 | tf_op jit(solution)/shard_map/all_to_all | solution.py:185
  35.6 1.2 reduce-window.6
  37.2 2.6 %scatter_custom_fusion = s32[1024]{0:T(1024)S(1)} fusion(s32[512]{0:T(512)S(1)} %bitcast.171, s32[512]{0:T(512)S(1)} %iota.82, s32[]{:T(128)} %constant.156.clone.1), kind=kCustom, calls=%fused_computation.194 | custom fusion | bytes 4100 | tf_op jit(solution)/shard_map/scatter | solution.py:183
  39.9 9.1 %all-to-all-done = f32[32,1,3072]{2,1,0:T(1,128)S(1)} async-done(((f32[32,1,3072]{2,1,0:T(1,128)}), f32[32,1,3072]{2,1,0:T(1,128)S(1)}, u32[]{:S(2)}, u32[]{:S(2)}) %all-to-all-start) | async-done | bytes 393248 | tf_op jit(solution)/shard_map/all_to_all | solution.py:185
  49.5 1.5 reduce.18
  51.0 1.6 reshape.1632
  52.6 2.1 %gather_fusion.1 = f32[512,2,48]{2,1,0:T(2,128)S(1)} fusion(f32[2,48,1024]{1,0,2:T(2,128)S(1)} %bitcast.168, s32[1024]{0:T(1024)S(1)} %pad_clamp_fusion), kind=kCustom, calls=%fused_computation.1 | custom fusion | bytes 395264 | tf_op jit(solution)/shard_map/gather | solution.py:192
  55.0 111.0 %while.14 = (s32[]{:T(128)}, f32[8,2,1,16,768]{4,3,0,1,2:T(8,128)}, f32[8,2,1,48,64]{3,4,1,2,0:T(8,128)S(1)}, s32[8]{0:T(128)S(1)}, s32[8]{0:T(128)S(1)}, /*inde...) while((s32[]{:T(128)}, f32[8,2,1,16,768]{4,3,0,1,2:T(8,128)}, ...), condition=%wide.region_8.9_spmd, body=%wide.region_3.8_spmd.sunk | while | flops 5484184 | bytes 18067664 | solution.py:205
  55.0 0.6 dynamic_slice.92
  57.5 0.6 dynamic_slice.93
  58.1 1.4 fusion.186
  59.8 0.7 compare_convert_fusion.2
  63.0 0.9 broadcast_divide_fusion.6
  68.2 0.7 bitcast_dynamic-update-slice_fusion.2
  71.4 0.6 dynamic_slice.93
  72.0 1.4 fusion.186
  73.7 0.7 compare_convert_fusion.2
  76.9 0.9 broadcast_divide_fusion.6
  82.1 0.7 bitcast_dynamic-update-slice_fusion.2
  85.8 1.4 fusion.186
  87.6 0.7 compare_convert_fusion.2
  90.8 0.9 broadcast_divide_fusion.6
  95.9 0.7 bitcast_dynamic-update-slice_fusion.2
  99.1 0.6 dynamic_slice.93
  99.7 1.4 fusion.186
  101.4 0.7 compare_convert_fusion.2
  104.6 0.9 broadcast_divide_fusion.6
  109.8 0.7 bitcast_dynamic-update-slice_fusion.2
  113.0 0.6 dynamic_slice.93
  113.6 1.4 fusion.186
  115.3 0.7 compare_convert_fusion.2
  118.5 0.9 broadcast_divide_fusion.6
  123.7 0.7 bitcast_dynamic-update-slice_fusion.2
  126.8 0.6 dynamic_slice.93
  127.4 1.4 fusion.186
  129.2 0.7 compare_convert_fusion.2
  132.4 0.9 broadcast_divide_fusion.6
  137.5 0.7 bitcast_dynamic-update-slice_fusion.2
  140.7 0.6 dynamic_slice.93
  141.3 1.4 fusion.186
  143.0 0.7 compare_convert_fusion.2
  146.2 0.9 broadcast_divide_fusion.6
  151.4 0.7 bitcast_dynamic-update-slice_fusion.2
  154.6 0.6 dynamic_slice.93
  155.2 1.4 fusion.186
  156.9 0.7 compare_convert_fusion.2
  160.1 0.9 broadcast_divide_fusion.6
  165.3 0.7 bitcast_dynamic-update-slice_fusion.2
  166.7 2.8 %gather_fusion.2 = f32[1024,96]{1,0:T(8,128)S(1)} fusion(f32[513,96]{1,0:T(8,128)S(1)} %concatenate.543, s32[1024]{0:T(1024)S(1)} %fusion.100), kind=kCustom, calls=%fused_computation.2 | custom fusion | bytes 790528 | tf_op jit(solution)/shard_map/gather | solution.py:216
  170.2 2.6 %reshape.1633 = f32[32,1,3072]{2,1,0:T(1,128)} reshape(f32[1024,2,48]{2,1,0:T(2,128)S(1)} %bitcast.159) | data formatting | bytes 786432
  172.8 2.8 %all-to-all-start.1 = ((f32[32,1,3072]{2,1,0:T(1,128)}), f32[32,1,3072]{2,1,0:T(1,128)S(1)}, u32[]{:S(2)}, u32[]{:S(2)}) async-start(f32[32,1,3072]{2,1,0:T(1,128)} %reshape.1633), calls=%async_computation.1 | async-start | bytes 786432 | tf_op jit(solution)/shard_map/all_to_all | solution.py:217
  175.7 13.2 %all-to-all-done.1 = f32[32,1,3072]{2,1,0:T(1,128)S(1)} async-done(((f32[32,1,3072]{2,1,0:T(1,128)}), f32[32,1,3072]{2,1,0:T(1,128)S(1)}, u32[]{:S(2)}, u32[]{:S(2)}) %all-to-all-start.1) | async-done | bytes 393248 | tf_op jit(solution)/shard_map/all_to_all | solution.py:217
  189.0 1.5 reduce.19
  190.5 1.7 reshape.1634
  192.8 8.2 %scatter_custom_fusion.1 = f32[8192,96]{1,0:T(8,128)} fusion(s32[1024]{0:T(1024)S(1)} %bitcast.174, f32[1024,96]{1,0:T(8,128)S(1)} %copy.45, f32[]{:T(128)} %constant.152.clone.1), kind=kCustom, calls=%fused_computation.172 | custom fusion | flops 98304 | bytes 3145732 | tf_op jit(solution)/shard_map/scatter-add | solution.py:223
  201.0 5.3 %copy.46 = f32[96,8192]{1,0:T(8,128)} copy(f32[96,8192]{0,1:T(8,128)} %bitcast.155) | data formatting | bytes 6291456 | tf_op jit(solution)/shard_map/transpose | solution.py:225
  (638 shorter events, 63.6 us)
Async XLA Ops:
  19.8 15.6 %copy-start.2 = (s32[8,64]{1,0:T(8,128)S(1)}, s32[8,64]{1,0:T(8,128)}, u32[]{:S(2)}) copy-start(s32[8,64]{1,0:T(8,128)} %param.14) | copy-start | bytes 6148
  21.7 33.3 %copy-start = (bf16[8,16,768]{2,1,0:T(8,128)(2,1)S(1)}, bf16[8,16,768]{2,1,0:T(8,128)(2,1)}, u32[]{:S(2)}) copy-start(bf16[8,16,768]{2,1,0:T(8,128)(2,1)} %param.11) | copy-start | bytes 589828
  21.7 33.3 %copy-start.3 = (s32[8]{0:T(128)S(1)}, s32[8]{0:T(128)}, u32[]{:S(2)}) copy-start(s32[8]{0:T(128)} %param.13) | copy-start | bytes 100
  28.1 20.8 %all-to-all-start = ((f32[32,1,3072]{2,1,0:T(1,128)}), f32[32,1,3072]{2,1,0:T(1,128)S(1)}, u32[]{:S(2)}, u32[]{:S(2)}) async-start(f32[32,1,3072]{2,1,0:T(1,128)} %reshape.1631), calls=%async_computation | async-start | bytes 786432 | tf_op jit(solution)/shard_map/all_to_all | solution.py:185
  166.7 9.0 %copy-start.1 = (s32[1,32,32]{2,1,0:T(8,128)S(1)}, s32[1,32,32]{2,1,0:T(8,128)}, u32[]{:S(2)}) copy-start(s32[1,32,32]{2,1,0:T(8,128)} %param.15) | copy-start | bytes 12292
  172.8 16.1 %all-to-all-start.1 = ((f32[32,1,3072]{2,1,0:T(1,128)}), f32[32,1,3072]{2,1,0:T(1,128)S(1)}, u32[]{:S(2)}, u32[]{:S(2)}) async-start(f32[32,1,3072]{2,1,0:T(1,128)} %reshape.1633), calls=%async_computation.1 | async-start | bytes 786432 | tf_op jit(solution)/shard_map/all_to_all | solution.py:217
where the time goes:
time: 208 us; the launch traced here: 206 us
  local copies, waits for them, and re-layouts  98.7 us (47%)
  other arithmetic  56.3 us (27%)
  waiting for transfers between devices  22.3 us (11%)
  loops' own time  18 us (9%)
  starting transfers between devices  10.1 us (5%)
    unnamed x13, local copies, waits for them, and re-layouts  19.2 us
    another operation x1, loops' own time, per_device(): adjoint, forces = lax.map(solve_one, jnp.arange(sub_local))  18 us
    all_to_all x1, waiting for transfers between devices, per_device(): lax.all_to_all(outbound, ('grp', 'sub'), split_axis=2, concat_axis=2, til...  13.2 us
    mul x8, other arithmetic, flat_coeffs(): (FIBER_COND * (1.0 - cos_square) + TRANSVERSE * cos_square) * active_mask  11.1 us
    div x32, other arithmetic, solve_cells(): direction = residual / (CHEB_CENTER * diagonal)  10.9 us
    all_to_all x1, waiting for transfers between devices, per_device(): lax.all_to_all(picked.reshape(case_count, ply_count, slot_total), ('grp',...  9.06 us
    gather x3, local copies, waits for them, and re-layouts, per_device(): shell_state[:, :, jnp.where(live_slot, node_table, 0)]  8.76 us
    scatter-add x1, other arithmetic, per_device(): node_rows = jnp.zeros((node_local, case_count * ply_count), jnp.float32)....  8.18 us
  transfers between devices with their start and end apart: 2, of which 2 were waited for; matrix products, arithmetic and copies ran while one was open for 2% of the time, Pallas kernels for 0%

commit v1 on v0

--- a/solution.py
+++ b/solution.py
@@ -214,7 +214,15 @@
         [force_rows, jnp.zeros((1, case_count * ply_count), jnp.float32)], axis=0
     )
     outbound = padded_rows[slot_source].T.reshape(case_count, ply_count, slot_total)
-    returned = lax.all_to_all(outbound, ("grp", "sub"), split_axis=2, concat_axis=2, tiled=True)
+    returned = jnp.concatenate(
+        lax.all_to_all(
+            jnp.stack(jnp.split(outbound, lax.axis_size(("grp", "sub")), axis=2)),
+            ("grp", "sub"),
+            0,
+            0,
+        ),
+        axis=2,
+    )
     returned_rows = returned.reshape(case_count * ply_count, slot_total).T
     target = jnp.where(live_slot, node_table, node_local).reshape(slot_total)
     node_rows = (

time: 208 us -> 215 us (1.034)
  waiting for transfers between devices: 22.3 us -> 26.6 us
  local copies, waits for them, and re-layouts: 98.7 us -> 101 us
    all_to_all x1, waiting for transfers between devices: 9.06 us -> 13.3 us  [per_device(): lax.all_to_all(picked.reshape(case_count, ply_count, slot_total), ('grp',...]
    unnamed x13 -> x42, local copies, waits for them, and re-layouts: 19.2 us -> 19.1 us
  transfers between devices with their start and end apart: 2 -> 2, of which waited for: 2 -> 2; matrix products, arithmetic and copies ran while one was open for 2% -> 0% of each run, Pallas kernels for 0% -> 0%
where the time goes in v1:
time: 215 us; the launch traced here: 213 us
  local copies, waits for them, and re-layouts  101 us (47%)
  other arithmetic  56.5 us (26%)
  waiting for transfers between devices  26.6 us (12%)
  loops' own time  18.1 us (8%)
  starting transfers between devices  10.3 us (5%)
    unnamed x42, local copies, waits for them, and re-layouts  19.1 us
    another operation x1, loops' own time, per_device(): adjoint, forces = lax.map(solve_one, jnp.arange(sub_local))  18.1 us
    all_to_all x1, waiting for transfers between devices, per_device(): lax.all_to_all(picked.reshape(case_count, ply_count, slot_total), ('grp',...  13.3 us
    all_to_all x1, waiting for transfers between devices, per_device(): lax.all_to_all(jnp.stack(jnp.split(outbound, lax.axis_size(('grp', 'sub')...  13.2 us
    mul x8, other arithmetic, flat_coeffs(): (FIBER_COND * (1.0 - cos_square) + TRANSVERSE * cos_square) * active_mask  11.1 us
    div x32, other arithmetic, solve_cells(): direction = residual / (CHEB_CENTER * diagonal)  10.7 us
    gather x3, local copies, waits for them, and re-layouts, per_device(): shell_state[:, :, jnp.where(live_slot, node_table, 0)]  8.76 us
    scatter-add x1, other arithmetic, per_device(): node_rows = jnp.zeros((node_local, case_count * ply_count), jnp.float32)....  8.21 us
  transfers between devices with their start and end apart: 2, of which 2 were waited for; matrix products, arithmetic and copies ran while one was open for 0% of the time, Pallas kernels for 0%

profile of v1, /device:TPU:0, one launch (start us, length us, event | category | flops | bytes accessed | tf_op | source)
XLA Modules:
  0.0 212.9 jit_solution(11566306725449504400)
XLA Ops:
  0.6 0.8 eq.111
  1.4 0.8 eq.107
  2.2 0.7 broadcast_multiply_fusion.1
  2.8 0.7 compare_select_fusion.2
  3.6 0.7 broadcast_compare_fusion
  4.3 1.2 reduce-window.6
  5.9 10.7 %copy.32 = f32[2,48,8192]{1,0,2:T(2,128)} copy(f32[2,48,8192]{2,1,0:T(8,128)} %param.9) | data formatting | bytes 6291456 | tf_op args[0]
  16.7 2.4 %scatter_custom_fusion = s32[1024]{0:T(1024)S(1)} fusion(s32[512]{0:T(512)S(1)} %bitcast.333, s32[512]{0:T(512)S(1)} %iota.82, s32[]{:T(128)} %constant.156.clone.1), kind=kCustom, calls=%fused_computation.259 | custom fusion | bytes 4100 | tf_op jit(solution)/shard_map/scatter | solution.py:183
  19.2 6.9 %gather_fusion = f32[1024,2,48]{2,1,0:T(2,128)S(1)} fusion(f32[2,48,8192]{1,0,2:T(2,128)} %copy.32, s32[1024]{0:T(1024)S(1)} %get-tuple-element.290), kind=kCustom, calls=%fused_computation | custom fusion | bytes 790528 | tf_op jit(solution)/shard_map/gather | solution.py:174
  26.1 1.0 copy.46
  27.1 0.9 copy.47
  28.1 3.7 %bitcast_select_fusion = f32[2,48,1024]{1,0,2:T(2,128)S(1)} fusion(f32[2,48,32,32]{1,0,3,2:T(2,128)S(1)} %copy.47, pred[1024]{0:T(1024)(128)(4,1)S(1)} %ge.30), kind=kLoop, calls=%fused_computation.174 | loop fusion | flops 98304 | bytes 787456 | tf_op jit(solution)/shard_map/jit(_where)/select_n | solution.py:173
  31.8 2.6 %reshape.1631 = f32[32,1,3072]{2,1,0:T(1,128)} reshape(f32[1024,2,48]{2,1,0:T(2,128)S(1)} %bitcast.325) | data formatting | bytes 786432
  34.4 7.5 %all-to-all-start = ((f32[32,1,3072]{2,1,0:T(1,128)}), f32[32,1,3072]{2,1,0:T(1,128)S(1)}, u32[]{:S(2)}, u32[]{:S(2)}) async-start(f32[32,1,3072]{2,1,0:T(1,128)} %reshape.1631), calls=%async_computation | async-start | bytes 786432 | tf_op jit(solution)/shard_map/all_to_all | solution.py:185
  41.9 13.3 %all-to-all-done = f32[32,1,3072]{2,1,0:T(1,128)S(1)} async-done(((f32[32,1,3072]{2,1,0:T(1,128)}), f32[32,1,3072]{2,1,0:T(1,128)S(1)}, u32[]{:S(2)}, u32[]{:S(2)}) %all-to-all-start) | async-done | bytes 393248 | tf_op jit(solution)/shard_map/all_to_all | solution.py:185
  55.8 1.5 reduce.18
  57.3 1.6 reshape.1632
  58.9 2.1 gather_fusion.1
  61.2 110.5 %while.14 = (s32[]{:T(128)}, f32[8,2,1,16,768]{4,3,0,1,2:T(8,128)}, f32[8,2,1,48,64]{3,4,1,2,0:T(8,128)S(1)}, s32[8]{0:T(128)S(1)}, s32[8]{0:T(128)S(1)}, /*inde...) while((s32[]{:T(128)}, f32[8,2,1,16,768]{4,3,0,1,2:T(8,128)}, ...), condition=%wide.region_8.9_spmd, body=%wide.region_3.8_spmd.sunk | while | flops 5484184 | bytes 18067664 | solution.py:205
  61.3 0.6 dynamic_slice.92
  64.4 1.4 fusion.187
  66.1 0.7 compare_convert_fusion.2
  69.3 0.9 broadcast_divide_fusion.6
  74.4 0.7 bitcast_dynamic-update-slice_fusion.2
  78.2 1.4 fusion.187
  79.9 0.7 compare_convert_fusion.2
  83.1 0.9 broadcast_divide_fusion.6
  88.2 0.7 bitcast_dynamic-update-slice_fusion.2
  92.0 1.4 fusion.187
  93.7 0.7 compare_convert_fusion.2
  96.9 0.9 broadcast_divide_fusion.6
  102.0 0.7 bitcast_dynamic-update-slice_fusion.2
  105.2 0.6 dynamic_slice.93
  105.8 1.4 fusion.187
  107.5 0.7 compare_convert_fusion.2
  110.7 0.9 broadcast_divide_fusion.6
  115.8 0.7 bitcast_dynamic-update-slice_fusion.2
  119.0 0.6 dynamic_slice.93
  119.6 1.4 fusion.187
  121.3 0.7 compare_convert_fusion.2
  124.5 0.9 broadcast_divide_fusion.6
  129.6 0.7 bitcast_dynamic-update-slice_fusion.2
  132.8 0.6 dynamic_slice.93
  133.4 1.4 fusion.187
  135.1 0.7 compare_convert_fusion.2
  138.4 0.9 broadcast_divide_fusion.6
  143.5 0.7 bitcast_dynamic-update-slice_fusion.2
  146.6 0.6 dynamic_slice.93
  147.2 1.4 fusion.187
  149.0 0.7 compare_convert_fusion.2
  152.2 0.9 broadcast_divide_fusion.6
  157.3 0.7 bitcast_dynamic-update-slice_fusion.2
  161.0 1.4 fusion.187
  162.8 0.7 compare_convert_fusion.2
  166.0 0.9 broadcast_divide_fusion.6
  171.1 0.7 bitcast_dynamic-update-slice_fusion.2
  172.5 2.8 %gather_fusion.2 = f32[1024,96]{1,0:T(8,128)S(1)} fusion(f32[513,96]{1,0:T(8,128)S(1)} %concatenate.543, s32[1024]{0:T(1024)S(1)} %get-tuple-element.289), kind=kCustom, calls=%fused_computation.2 | custom fusion | bytes 790528 | tf_op jit(solution)/shard_map/gather | solution.py:216
  178.0 1.7 reshape.1633
  179.8 2.8 %all-to-all-start.1 = ((f32[32,1,3072]{2,1,0:T(1,128)}), f32[32,1,3072]{2,1,0:T(1,128)S(1)}, u32[]{:S(2)}, u32[]{:S(2)}) async-start(f32[32,1,3072]{2,1,0:T(1,128)} %reshape.1633), calls=%async_computation.1 | async-start | bytes 786432 | tf_op jit(solution)/shard_map/all_to_all | solution.py:218
  182.7 13.2 %all-to-all-done.1 = f32[32,1,3072]{2,1,0:T(1,128)S(1)} async-done(((f32[32,1,3072]{2,1,0:T(1,128)}), f32[32,1,3072]{2,1,0:T(1,128)S(1)}, u32[]{:S(2)}, u32[]{:S(2)}) %all-to-all-start.1) | async-done | bytes 393248 | tf_op jit(solution)/shard_map/all_to_all | solution.py:218
  195.9 1.5 reduce.19
  198.0 0.8 copy.44
  199.4 8.2 %scatter_custom_fusion.1 = f32[8192,96]{1,0:T(8,128)} fusion(s32[1024]{0:T(1024)S(1)} %bitcast.336, f32[]{:T(128)} %constant.152.clone.1, f32[96,1024]{0,1:T(8,128)S(1)} %reshape_reshape.3), kind=kCustom, calls=%fused_computation.172 | custom fusion | flops 98304 | bytes 3670020 | tf_op jit(solution)/shard_map/scatter-add | solution.py:231
  207.6 5.3 %copy.45 = f32[96,8192]{1,0:T(8,128)} copy(f32[96,8192]{0,1:T(8,128)} %bitcast.288) | data formatting | bytes 6291456 | tf_op jit(solution)/shard_map/transpose | solution.py:233
  (668 shorter events, 67.0 us)
Async XLA Ops:
  34.4 20.8 %all-to-all-start = ((f32[32,1,3072]{2,1,0:T(1,128)}), f32[32,1,3072]{2,1,0:T(1,128)S(1)}, u32[]{:S(2)}, u32[]{:S(2)}) async-start(f32[32,1,3072]{2,1,0:T(1,128)} %reshape.1631), calls=%async_computation | async-start | bytes 786432 | tf_op jit(solution)/shard_map/all_to_all | solution.py:185
  57.3 4.0 %copy-start = (bf16[8,16,768]{2,1,0:T(8,128)(2,1)S(1)}, bf16[8,16,768]{2,1,0:T(8,128)(2,1)}, u32[]{:S(2)}) copy-start(bf16[8,16,768]{2,1,0:T(8,128)(2,1)} %param.11) | copy-start | bytes 589828
  57.3 4.0 %copy-start.2 = (s32[8]{0:T(128)S(1)}, s32[8]{0:T(128)}, u32[]{:S(2)}) copy-start(s32[8]{0:T(128)} %param.13) | copy-start | bytes 100
  178.0 4.6 %copy-start.1 = (s32[1,32,32]{2,1,0:T(8,128)S(1)}, s32[1,32,32]{2,1,0:T(8,128)}, u32[]{:S(2)}) copy-start(s32[1,32,32]{2,1,0:T(8,128)} %param.15) | copy-start | bytes 12292
  179.8 16.1 %all-to-all-start.1 = ((f32[32,1,3072]{2,1,0:T(1,128)}), f32[32,1,3072]{2,1,0:T(1,128)S(1)}, u32[]{:S(2)}, u32[]{:S(2)}) async-start(f32[32,1,3072]{2,1,0:T(1,128)} %reshape.1633), calls=%async_computation.1 | async-start | bytes 786432 | tf_op jit(solution)/shard_map/all_to_all | solution.py:218
